TPU v7x, 32 devices: a whole 2x2x4 slice. The times are simulated.
32 devices in a mesh: items: 16 (over z, y, core), seq: 2 (over x).
Axes of the slice: x: 2, y: 2, z: 4, core: 2. Of those that a mesh axis runs over, the one named last changes fastest.
Arguments:
- tokens: bfloat16 [16, 1280, 1024], P('items', 'seq'), may hold values from -6 to 6
- cotangent: bfloat16 [16, 1280, 1024], P('items', 'seq'), may hold values from -6 to 6
- prompt_len: int32 [16], P('items'), may hold values from 150 to 600
- section_ids: int32 [16], P('items'), may hold values from 0 to 7
- section_table: bfloat16 [8, 1024], replicated, may hold values from -6 to 6
- w_query: bfloat16 [1024, 1024], P('items'), may hold values from -0.1875 to 0.1875
- w_key: bfloat16 [1024, 1024], P('items'), may hold values from -0.1875 to 0.1875
- w_value: bfloat16 [1024, 1024], P('items'), may hold values from -0.1875 to 0.1875
- w_out: bfloat16 [1024, 1024], P('items'), may hold values from -4 to 4
- w_up: bfloat16 [1024, 4096], P('items'), may hold values from -0.1875 to 0.1875
- w_down: bfloat16 [4096, 1024], P('items'), may hold values from -0.09375 to 0.09375
- w_ada_one: bfloat16 [1024, 2048], P('items'), may hold values from -0.09375 to 0.09375
- w_ada_two: bfloat16 [1024, 2048], P('items'), may hold values from -0.09375 to 0.09375
Outputs:
- layer_out: bfloat16 [16, 1280, 1024], P('items', 'seq')
- input_grad: float32 [16, 1280, 1024], P('items', 'seq')
- grad_query: float32 [1024, 1024], P(('items', 'seq'))
- grad_key: float32 [1024, 1024], P(('items', 'seq'))
- grad_value: float32 [1024, 1024], P(('items', 'seq'))
- grad_out: float32 [1024, 1024], P(('items', 'seq'))
- grad_up: float32 [1024, 4096], P(('items', 'seq'))
- grad_down: float32 [4096, 1024], P(('items', 'seq'))
- grad_ada_one: float32 [1024, 2048], P(('items', 'seq'))
- grad_ada_two: float32 [1024, 2048], P(('items', 'seq'))
- grad_table: float32 [8, 1024], P(None, ('items', 'seq'))
Inputs may be any that keep to these rules, and one draw needn't show every extreme that they name: `prompt_len`: prompt frames at and past an item's length are padding. `section_ids`: the number of items per section is uneven across sections.
All inputs are finite; a program needn't handle non-finite values.
Results may differ from a plain program's by a relative error of at most 0.019.
Values may be sent and summed in bfloat16 or wider, within the bound.
No kernel may reach another device: no remote copies, remote signals or barrier semaphores. Data moves between devices by JAX's collectives and lax.ppermute only.
A program may use at most 384 MiB of HBM per device.

v0:
```python
from functools import partial
import math
import jax
import jax.numpy as jnp
from jax import lax
from jax.sharding import PartitionSpec as P

HEADS = 16
HEAD_DIM = 64
PROMPT = 640
EPSILON = 1e-05
MASKED = -1e30


def exact(left, right):
    return jnp.dot(left, right, precision=lax.Precision.HIGHEST)


def dot_rows(left, right):
    return lax.dot_general(
        left, right, (((0,), (0,)), ((), ())), preferred_element_type=jnp.float32
    )


def dot_last(left, right):
    return lax.dot_general(
        left, right, (((1,), (1,)), ((), ())), preferred_element_type=jnp.float32
    )


def ada_norm(values, ada):
    width = values.shape[-1]
    centred = values - jnp.mean(values, axis=-1, keepdims=True)
    spread = jnp.mean(centred * centred, axis=-1, keepdims=True)
    normed = centred * lax.rsqrt(spread + EPSILON)
    return (1.0 + ada[:, None, :width]) * normed + ada[:, None, width:]


def split_heads(block):
    return block.reshape(block.shape[0], HEADS, HEAD_DIM)


def frames_major(grad, dim, items_count, seq_count):
    shape = grad.shape
    piece = shape[dim] // (items_count * seq_count)
    parted = grad.reshape(shape[:dim] + (items_count, seq_count, piece) + shape[dim + 1 :])
    return jnp.swapaxes(parted, dim, dim + 1).reshape(shape)


def shards(
    tokens,
    cotangent,
    prompt_len,
    section_ids,
    section_table,
    w_query,
    w_key,
    w_value,
    w_out,
    w_up,
    w_down,
    w_ada_one,
    w_ada_two,
):
    full_query, full_key, full_value, full_out, full_up, full_down, full_ada_one, full_ada_two = (
        lax.all_gather(w_query, "items", axis=0, tiled=True),
        lax.all_gather(w_key, "items", axis=0, tiled=True),
        lax.all_gather(w_value, "items", axis=0, tiled=True),
        lax.all_gather(w_out, "items", axis=0, tiled=True),
        lax.all_gather(w_up, "items", axis=0, tiled=True),
        lax.all_gather(w_down, "items", axis=0, tiled=True),
        lax.all_gather(w_ada_one, "items", axis=0, tiled=True),
        lax.all_gather(w_ada_two, "items", axis=0, tiled=True),
    )
    batch, rows, width = tokens.shape
    items_count = lax.axis_size("items")
    seq_count = lax.axis_size("seq")
    frames_all = rows * seq_count
    scale = 1.0 / math.sqrt(HEAD_DIM)
    position = lax.axis_index("seq") * rows + jnp.arange(rows)
    key_place = jnp.arange(frames_all)
    inputs = tokens.astype(jnp.float32)
    choose = (section_ids[:, None] == jnp.arange(section_table.shape[0])[None, :]).astype(
        jnp.float32
    )
    cond = exact(choose, section_table.astype(jnp.float32))
    ada_one_w = full_ada_one.astype(jnp.float32)
    ada_two_w = full_ada_two.astype(jnp.float32)
    ada_one = exact(cond, ada_one_w)
    ada_two = exact(cond, ada_two_w)
    normed_one, back_one = jax.vjp(ada_norm, inputs, ada_one)
    low_one = normed_one.astype(jnp.bfloat16).reshape(-1, width)
    query = (
        jnp.dot(low_one, full_query, preferred_element_type=jnp.float32)
        .astype(jnp.bfloat16)
        .reshape(batch, rows, width)
    )
    keys_here = (
        jnp.dot(low_one, full_key, preferred_element_type=jnp.float32)
        .astype(jnp.bfloat16)
        .reshape(batch, rows, width)
    )
    values_here = (
        jnp.dot(low_one, full_value, preferred_element_type=jnp.float32)
        .astype(jnp.bfloat16)
        .reshape(batch, rows, width)
    )
    keys_all, values_all = (
        lax.all_gather(keys_here, "seq", axis=1, tiled=True),
        lax.all_gather(values_here, "seq", axis=1, tiled=True),
    )

    def masked_scores(query_item, keys_item, length, query_place, key_spot):
        raw = (
            jnp.einsum(
                "qhd,khd->hqk",
                split_heads(query_item),
                split_heads(keys_item),
                preferred_element_type=jnp.float32,
            )
            * scale
        )
        allowed = (key_spot[None, :] < length) | (key_spot[None, :] >= PROMPT) & (
            query_place[:, None] >= PROMPT
        )
        return jnp.where(allowed[None], raw, MASKED)

    def attend(packed):
        query_item, keys_item, values_item, length = packed
        scores = masked_scores(query_item, keys_item, length, position, key_place)
        peak = jnp.max(scores, axis=-1, keepdims=True)
        expo = jnp.exp(scores - peak)
        total = jnp.sum(expo, axis=-1, keepdims=True)
        probs = (expo / total).astype(jnp.bfloat16)
        mixed_item = jnp.einsum(
            "hqk,khd->qhd", probs, split_heads(values_item), preferred_element_type=jnp.float32
        )
        return (
            mixed_item.astype(jnp.bfloat16).reshape(rows, width),
            (peak + jnp.log(total))[..., 0],
        )

    mixed, log_total = lax.map(attend, (query, keys_all, values_all, prompt_len))
    mixed_flat = mixed.reshape(-1, width)
    attended = inputs + jnp.dot(mixed_flat, full_out, preferred_element_type=jnp.float32).reshape(
        batch, rows, width
    )
    normed_two, back_two = jax.vjp(ada_norm, attended, ada_two)
    low_two = normed_two.astype(jnp.bfloat16).reshape(-1, width)
    upward = jnp.dot(low_two, full_up, preferred_element_type=jnp.float32)
    active, gelu_back = jax.vjp(partial(jax.nn.gelu, approximate=False), upward)
    active_low = active.astype(jnp.bfloat16)
    layer_out = (
        attended
        + jnp.dot(active_low, full_down, preferred_element_type=jnp.float32).reshape(
            batch, rows, width
        )
    ).astype(jnp.bfloat16)
    grad_top = cotangent.astype(jnp.float32)
    grad_low = cotangent.reshape(-1, width)
    grad_down = dot_rows(active_low, grad_low)
    (grad_upward,) = gelu_back(dot_last(grad_low, full_down))
    upward_low = grad_upward.astype(jnp.bfloat16)
    grad_up = dot_rows(low_two, upward_low)
    grad_normed_two = dot_last(upward_low, full_up).reshape(batch, rows, width)
    back_mid, grad_ada_two_rows = back_two(grad_normed_two)
    grad_attended = grad_top + back_mid
    grad_ada_two = exact(cond.T, grad_ada_two_rows)
    attended_low = grad_attended.astype(jnp.bfloat16).reshape(-1, width)
    grad_out = dot_rows(mixed_flat, attended_low)
    grad_mixed = dot_last(attended_low, full_out).astype(jnp.bfloat16).reshape(batch, rows, width)

    def score_grads(
        query_item, keys_item, values_item, length, log_item, grad_item, query_place, key_spot
    ):
        scores = masked_scores(query_item, keys_item, length, query_place, key_spot)
        probs = jnp.exp(scores - log_item[..., None])
        grad_heads = split_heads(grad_item)
        grad_probs = jnp.einsum(
            "qhd,khd->hqk", grad_heads, split_heads(values_item), preferred_element_type=jnp.float32
        )
        inner = jnp.sum(probs * grad_probs, axis=-1, keepdims=True)
        grad_scores = (probs * (grad_probs - inner)).astype(jnp.bfloat16)
        return (probs, grad_heads, grad_scores, inner[..., 0])

    def attend_back(packed):
        query_item, keys_item, values_item, length, log_item, grad_item = packed
        probs, grad_heads, grad_scores, inner = score_grads(
            query_item, keys_item, values_item, length, log_item, grad_item, position, key_place
        )
        grad_query_item = (
            jnp.einsum(
                "hqk,khd->qhd",
                grad_scores,
                split_heads(keys_item),
                preferred_element_type=jnp.float32,
            )
            * scale
        )
        grad_keys_item = (
            jnp.einsum(
                "hqk,qhd->khd",
                grad_scores,
                split_heads(query_item),
                preferred_element_type=jnp.float32,
            )
            * scale
        )
        grad_values_item = jnp.einsum(
            "hqk,qhd->khd",
            probs.astype(jnp.bfloat16),
            grad_heads,
            preferred_element_type=jnp.float32,
        )
        return (
            grad_query_item.reshape(rows, width),
            grad_keys_item.reshape(frames_all, width),
            grad_values_item.reshape(frames_all, width),
        )

    grad_query_rows, grad_keys_all, grad_values_all = lax.map(
        attend_back, (query, keys_all, values_all, prompt_len, log_total, grad_mixed)
    )
    grad_keys_here, grad_values_here = (
        lax.psum_scatter(
            grad_keys_all.astype(jnp.bfloat16), "seq", scatter_dimension=1, tiled=True
        ).astype(jnp.float32),
        lax.psum_scatter(
            grad_values_all.astype(jnp.bfloat16), "seq", scatter_dimension=1, tiled=True
        ).astype(jnp.float32),
    )
    query_low = grad_query_rows.astype(jnp.bfloat16).reshape(-1, width)
    keys_low = grad_keys_here.astype(jnp.bfloat16).reshape(-1, width)
    values_low = grad_values_here.astype(jnp.bfloat16).reshape(-1, width)
    grad_query = dot_rows(low_one, query_low)
    grad_key = dot_rows(low_one, keys_low)
    grad_value = dot_rows(low_one, values_low)
    grad_normed_one = (
        dot_last(query_low, full_query)
        + dot_last(keys_low, full_key)
        + dot_last(values_low, full_value)
    )
    back_in, grad_ada_one_rows = back_one(grad_normed_one.reshape(batch, rows, width))
    input_grad = grad_attended + back_in
    grad_ada_one = exact(cond.T, grad_ada_one_rows)
    grad_cond = exact(grad_ada_one_rows, ada_one_w.T) + exact(grad_ada_two_rows, ada_two_w.T)
    grad_table = exact(choose.T, grad_cond)
    table_t = frames_major(grad_table, 1, items_count, seq_count)
    part_query = frames_major(grad_query, 0, items_count, seq_count)
    part_key = frames_major(grad_key, 0, items_count, seq_count)
    part_value = frames_major(grad_value, 0, items_count, seq_count)
    part_out = frames_major(grad_out, 0, items_count, seq_count)
    part_ada_one = frames_major(grad_ada_one, 0, items_count, seq_count)
    part_up = frames_major(grad_up, 0, items_count, seq_count)
    part_down = frames_major(grad_down, 0, items_count, seq_count)
    part_ada_two = frames_major(grad_ada_two, 0, items_count, seq_count)
    (
        seq_query,
        seq_key,
        seq_value,
        seq_out,
        seq_up,
        seq_down,
        seq_ada_one,
        seq_ada_two,
        seq_table,
    ) = (
        lax.psum_scatter(
            part_query.astype(jnp.bfloat16), "seq", scatter_dimension=0, tiled=True
        ).astype(jnp.float32),
        lax.psum_scatter(
            part_key.astype(jnp.bfloat16), "seq", scatter_dimension=0, tiled=True
        ).astype(jnp.float32),
        lax.psum_scatter(
            part_value.astype(jnp.bfloat16), "seq", scatter_dimension=0, tiled=True
        ).astype(jnp.float32),
        lax.psum_scatter(
            part_out.astype(jnp.bfloat16), "seq", scatter_dimension=0, tiled=True
        ).astype(jnp.float32),
        lax.psum_scatter(
            part_up.astype(jnp.bfloat16), "seq", scatter_dimension=0, tiled=True
        ).astype(jnp.float32),
        lax.psum_scatter(
            part_down.astype(jnp.bfloat16), "seq", scatter_dimension=0, tiled=True
        ).astype(jnp.float32),
        lax.psum_scatter(
            part_ada_one.astype(jnp.bfloat16), "seq", scatter_dimension=0, tiled=True
        ).astype(jnp.float32),
        lax.psum_scatter(
            part_ada_two.astype(jnp.bfloat16), "seq", scatter_dimension=0, tiled=True
        ).astype(jnp.float32),
        lax.psum_scatter(
            table_t.astype(jnp.bfloat16), "seq", scatter_dimension=1, tiled=True
        ).astype(jnp.float32),
    )
    (
        grad_query,
        grad_key,
        grad_value,
        grad_out,
        grad_up,
        grad_down,
        grad_ada_one,
        grad_ada_two,
        grad_table,
    ) = (
        lax.psum_scatter(
            seq_query.astype(jnp.bfloat16), "items", scatter_dimension=0, tiled=True
        ).astype(jnp.float32),
        lax.psum_scatter(
            seq_key.astype(jnp.bfloat16), "items", scatter_dimension=0, tiled=True
        ).astype(jnp.float32),
        lax.psum_scatter(
            seq_value.astype(jnp.bfloat16), "items", scatter_dimension=0, tiled=True
        ).astype(jnp.float32),
        lax.psum_scatter(
            seq_out.astype(jnp.bfloat16), "items", scatter_dimension=0, tiled=True
        ).astype(jnp.float32),
        lax.psum_scatter(
            seq_up.astype(jnp.bfloat16), "items", scatter_dimension=0, tiled=True
        ).astype(jnp.float32),
        lax.psum_scatter(
            seq_down.astype(jnp.bfloat16), "items", scatter_dimension=0, tiled=True
        ).astype(jnp.float32),
        lax.psum_scatter(
            seq_ada_one.astype(jnp.bfloat16), "items", scatter_dimension=0, tiled=True
        ).astype(jnp.float32),
        lax.psum_scatter(
            seq_ada_two.astype(jnp.bfloat16), "items", scatter_dimension=0, tiled=True
        ).astype(jnp.float32),
        lax.psum_scatter(
            seq_table.astype(jnp.bfloat16), "items", scatter_dimension=1, tiled=True
        ).astype(jnp.float32),
    )
    return (
        layer_out,
        input_grad,
        grad_query,
        grad_key,
        grad_value,
        grad_out,
        grad_up,
        grad_down,
        grad_ada_one,
        grad_ada_two,
        grad_table,
    )


def solution(mesh):
    return jax.shard_map(
        shards,
        mesh=mesh,
        in_specs=(
            P("items", "seq", None),
            P("items", "seq", None),
            P("items"),
            P("items"),
            P(),
            P("items", None),
            P("items", None),
            P("items", None),
            P("items", None),
            P("items", None),
            P("items", None),
            P("items", None),
            P("items", None),
        ),
        out_specs=(
            P("items", "seq", None),
            P("items", "seq", None),
            P(("items", "seq"), None),
            P(("items", "seq"), None),
            P(("items", "seq"), None),
            P(("items", "seq"), None),
            P(("items", "seq"), None),
            P(("items", "seq"), None),
            P(("items", "seq"), None),
            P(("items", "seq"), None),
            P(None, ("items", "seq")),
        ),
        check_vma=False,
    )
```

profile of v0, /device:TPU:0, one launch (start us, length us, event | category | flops | bytes accessed | tf_op | source)
XLA Modules:
  0.0 1794.8 jit_solution(3981334618277993144)
XLA Ops:
  14.1 49.4 %all-gather.13.cloned.1.call-done = bf16[1024,2048]{1,0:T(8,128)(2,1)} async-done(((bf16[64,2048]{1,0:T(8,128)(2,1)}), bf16[1024,2048]{1,0:T(8,128)(2,1)}) %all-gather.13.cloned.1.call-update) | async-done | bytes 4194320 | tf_op jit(solution)/shard_map/all_gather | solution.py:72
  63.5 3.9 fusion.75
  67.4 38.1 %all-gather.19.cloned.1.call-done = bf16[1024,1024]{1,0:T(8,128)(2,1)} async-done(((bf16[64,1024]{1,0:T(8,128)(2,1)}), bf16[1024,1024]{1,0:T(8,128)(2,1)}) %all-gather.19.cloned.1.call-update) | async-done | bytes 2097168 | tf_op jit(solution)/shard_map/all_gather | solution.py:67
  105.6 4.2 convolution_convert_fusion.1
  109.9 38.1 %all-gather.15.cloned.1.call-done = bf16[1024,1024]{1,0:T(8,128)(2,1)} async-done(((bf16[64,1024]{1,0:T(8,128)(2,1)}), bf16[1024,1024]{1,0:T(8,128)(2,1)}) %all-gather.15.cloned.1.call-update) | async-done | bytes 2097168 | tf_op jit(solution)/shard_map/all_gather | solution.py:68
  148.0 4.2 convolution_convert_fusion.3
  155.7 43.8 %all-gather.23.cloned.1.call-done = bf16[1024,2048]{1,0:T(8,128)(2,1)} async-done(((bf16[64,2048]{1,0:T(8,128)(2,1)}), bf16[1024,2048]{1,0:T(8,128)(2,1)}) %all-gather.23.cloned.1.call-update) | async-done | bytes 4194320 | tf_op jit(solution)/shard_map/all_gather | solution.py:73
  199.5 3.9 fusion.73
  203.4 38.0 %all-gather.17.cloned.1.call-done = bf16[1024,1024]{1,0:T(8,128)(2,1)} async-done(((bf16[64,1024]{1,0:T(8,128)(2,1)}), bf16[1024,1024]{1,0:T(8,128)(2,1)}) %all-gather.17.cloned.1.call-update) | async-done | bytes 2097168 | tf_op jit(solution)/shard_map/all_gather | solution.py:66
  241.5 3.2 convolution_convert_fusion.2
  246.1 35.2 %all-gather.31.cloned.1.call-done = bf16[1280,1024]{1,0:T(8,128)(2,1)} async-done(((bf16[640,1024]{1,0:T(8,128)(2,1)}), bf16[1280,1024]{1,0:T(8,128)(2,1)}) %all-gather.31.cloned.1.call-update) | async-done | bytes 2621456 | tf_op jit(solution)/shard_map/all_gather | solution.py:109
  281.3 3.0 copy.60
  284.3 23.1 %fusion.93 = (f32[16,640]{1,0:T(8,128)S(1)}, f32[16,640,1280]{2,1,0:T(8,128)}) fusion(bf16[640,16,64]{0,2,1:T(8,128)(2,1)} %bitcast.284, bf16[1280,16,64]{0,2,1:T(8,128)(2,1)S(1)} %bitcast.278, pred[640,1280]{1,0:T(8,128)(4,1)S(1)} %and_or_fusion), kind=kOutput, calls=%fused_computation.153 | convolution fusion | flops 1717032960 | bytes 57221120 | tf_op jit(solution)/shard_map/while/body/eval_jaxpr/qhd,khd->hqk/dot_general | solution.py:115
  307.4 16.8 fusion
  324.2 4.4 copy.58
  328.6 20.2 %fusion.50 = bf16[16,64,640]{2,1,0:T(8,128)(2,1)S(1)} fusion(bf16[1280,16,64]{0,2,1:T(8,128)(2,1)} %bitcast.289, f32[16,640,1280]{2,1,0:T(8,128)} %get-tuple-element.90, f32[16,640]{1,0:T(8,128)S(1)} %fusion, f32[16,640]{1,0:T(8,128)S(1)} %get-tuple-element.89), kind=kOutput, calls=%fused_computation.97 | convolution fusion | flops 1717698560 | bytes 56442880 | tf_op jit(solution)/shard_map/while/body/eval_jaxpr/hqk,khd->qhd/dot_general | solution.py:135
  348.8 17.3 all-gather.21.cloned.1.call-done
  366.1 3.2 fusion.94
  371.3 70.7 %all-gather.25.cloned.1.call-done = bf16[1024,4096]{1,0:T(8,128)(2,1)} async-done(((bf16[64,4096]{1,0:T(8,128)(2,1)}), bf16[1024,4096]{1,0:T(8,128)(2,1)}) %all-gather.25.cloned.1.call-update) | async-done | bytes 8388624 | tf_op jit(solution)/shard_map/all_gather | solution.py:70
  442.0 32.4 %fusion.6 = (f32[640,4096]{1,0:T(8,128)}, f32[640,4096]{1,0:T(8,128)}) fusion(bf16[1024,4096]{1,0:T(8,128)(2,1)} %all-gather.25.cloned.1.call-done, f32[1024]{0:T(1024)S(1)} %bitcast.330, f32[640]{0:T(1024)S(1)} %fusion.78, f32[1,640,1024]{2,1,0:T(8,128)} %copy-done.6, f32[640]{0:T(1024)S(1)} %broadcast_multiply_fusion, f32[1024]{0:T(1024)S(1)} %bitcast.310), kind=kOutput, calls=%fused_computation.13 | convolution fusion | flops 5534515200 | bytes 31994880 | tf_op jit(solution)/shard_map/dot_general | solution.py:150
  474.4 42.8 %all-gather.27.cloned.1.call-done = bf16[4096,1024]{1,0:T(8,128)(2,1)} async-done(((bf16[256,1024]{1,0:T(8,128)(2,1)}), bf16[4096,1024]{1,0:T(8,128)(2,1)}) %all-gather.27.cloned.1.call-update) | async-done | bytes 8388624 | tf_op jit(solution)/shard_map/all_gather | solution.py:71
  517.2 16.8 add_convert_fusion
  533.9 10.2 fusion.95
  544.2 2.1 fusion.46
  552.4 38.6 %multiply_reduce_fusion = (f32[16,640]{1,0:T(8,128)S(1)}, f32[16,640,1280]{2,1,0:T(8,128)}) fusion(f32[16,640,1280]{2,1,0:T(8,128)} %get-tuple-element.90, f32[16,640]{1,0:T(8,128)S(1)} %log_add_fusion, bf16[640,16,64]{0,2,1:T(8,128)(2,1)S(1)} %bitcast.287, bf16[1280,16,64]{0,2,1:T(8,128)(2,1)} %bitcast.290), kind=kOutput, calls=%fused_computation.1 | convolution fusion | flops 1717032960 | bytes 108871680 | tf_op jit(solution)/shard_map/while/body/eval_jaxpr/qhd,khd->hqk/dot_general | solution.py:179
  591.0 42.2 %multiply_convert_fusion = bf16[16,640,1280]{2,1,0:T(8,128)(2,1)} fusion(f32[16,640,1280]{2,1,0:T(8,128)} %get-tuple-element.96, f32[16,640,1280]{2,1,0:T(8,128)} %get-tuple-element.90, f32[16,640]{1,0:T(8,128)S(1)} %get-tuple-element.95, f32[16,640]{1,0:T(8,128)S(1)} %log_add_fusion), kind=kLoop, calls=%fused_computation | loop fusion | flops 52428800 | bytes 131153920 | tf_op jit(solution)/shard_map/while/body/eval_jaxpr/convert_element_type | solution.py:183
  633.2 14.6 multiply_convert_fusion.5
  647.8 4.5 copy.62
  652.4 21.5 %fusion.36 = bf16[16,64,1280]{2,1,0:T(8,128)(2,1)} fusion(bf16[640,16,64]{0,2,1:T(8,128)(2,1)S(1)} %bitcast.288, f32[16,640,1280]{2,1,0:T(8,128)} %get-tuple-element.90, f32[16,640]{1,0:T(8,128)S(1)} %log_add_fusion), kind=kOutput, calls=%fused_computation.67 | convolution fusion | flops 1705246720 | bytes 56401920 | tf_op jit(solution)/shard_map/while/body/eval_jaxpr/hqk,qhd->khd/dot_general | solution.py:209
  673.9 4.5 copy.63
  678.5 5.7 fusion.69
  684.2 14.9 multiply_convert_fusion.6
  699.0 5.2 fusion.96
  704.2 4.4 fusion.56
  708.7 19.5 %reduce-scatter.25.cloned.1.call-done = bf16[1,640,1024]{2,1,0:T(8,128)(2,1)} async-done(((bf16[1,1280,1024]{2,1,0:T(8,128)(2,1)}), bf16[1,640,1024]{2,1,0:T(8,128)(2,1)}) %reduce-scatter.25.cloned.1.call-update) | async-done | bytes 1310736 | tf_op jit(solution)/shard_map/reduce_scatter | solution.py:228
  728.2 5.9 fusion.45
  734.7 2.5 fusion.43
  737.2 5.5 fusion.71
  744.1 3.5 convert_bitcast_fusion.2
  749.3 4.5 fusion.90
  759.3 1.8 convert_bitcast_fusion.5
  766.8 6.4 multiply_convert_fusion.2
  775.4 11.5 convert_bitcast_fusion.1
  786.9 7.8 copy.71
  794.7 24.6 %fusion.9 = bf16[4096,640]{0,1:T(8,128)(2,1)} fusion(f32[640,4096]{1,0:T(8,128)} %get-tuple-element.94), kind=kLoop, calls=%fused_computation.16 | loop fusion | flops 170393600 | bytes 15728640 | tf_op jit(solution)/shard_map/convert_element_type | solution.py:152
  819.4 7.9 copy.83
  827.3 11.6 convert_bitcast_fusion
  838.9 8.2 copy.73
  850.1 5.5 reduce-scatter.27.cloned.1.call-done
  855.6 34.0 %reduce-scatter.31.cloned.1.call-done = bf16[512,1024]{1,0:T(8,128)(2,1)} async-done(((bf16[1024,1024]{1,0:T(8,128)(2,1)}), bf16[512,1024]{1,0:T(8,128)(2,1)}) %reduce-scatter.31.cloned.1.call-update) | async-done | bytes 1048592 | tf_op jit(solution)/shard_map/reduce_scatter | solution.py:271
  889.7 56.4 %reduce-scatter.55.cloned.1.call-done = bf16[512,2048]{1,0:T(8,128)(2,1)} async-done(((bf16[1024,2048]{1,0:T(8,128)(2,1)}), bf16[512,2048]{1,0:T(8,128)(2,1)}) %reduce-scatter.55.cloned.1.call-update) | async-done | bytes 2097168 | tf_op jit(solution)/shard_map/reduce_scatter | solution.py:289
  946.2 56.7 %reduce-scatter.51.cloned.1.call-done = bf16[512,2048]{1,0:T(8,128)(2,1)} async-done(((bf16[1024,2048]{1,0:T(8,128)(2,1)}), bf16[512,2048]{1,0:T(8,128)(2,1)}) %reduce-scatter.51.cloned.1.call-update) | async-done | bytes 2097168 | tf_op jit(solution)/shard_map/reduce_scatter | solution.py:286
  1002.9 101.3 %reduce-scatter.43.cloned.1.call-done = bf16[512,4096]{1,0:T(8,128)(2,1)} async-done(((bf16[1024,4096]{1,0:T(8,128)(2,1)}), bf16[512,4096]{1,0:T(8,128)(2,1)}) %reduce-scatter.43.cloned.1.call-update) | async-done | bytes 4194320 | tf_op jit(solution)/shard_map/reduce_scatter | solution.py:280
  1104.5 101.4 %reduce-scatter.47.cloned.1.call-done = bf16[2048,1024]{1,0:T(8,128)(2,1)} async-done(((bf16[4096,1024]{1,0:T(8,128)(2,1)}), bf16[2048,1024]{1,0:T(8,128)(2,1)}) %reduce-scatter.47.cloned.1.call-update) | async-done | bytes 4194320 | tf_op jit(solution)/shard_map/reduce_scatter | solution.py:283
  1206.0 13.2 fusion.48
  1219.1 45.9 %reduce-scatter.61.cloned.1.call-done = bf16[32,8]{1,0:T(8,128)(2,1)} async-done(((bf16[512,8]{1,0:T(8,128)(2,1)}), bf16[32,8]{1,0:T(8,128)(2,1)}) %reduce-scatter.61.cloned.1.call-update) | async-done | bytes 528
  1266.4 58.7 %reduce-scatter.41.cloned.1.call-done = bf16[32,1024]{1,0:T(8,128)(2,1)} async-done(((bf16[512,1024]{1,0:T(8,128)(2,1)}), bf16[32,1024]{1,0:T(8,128)(2,1)}) %reduce-scatter.41.cloned.1.call-update) | async-done | bytes 65552 | tf_op jit(solution)/shard_map/reduce_scatter | solution.py:316
  1326.6 58.9 %reduce-scatter.37.cloned.1.call-done = bf16[32,1024]{1,0:T(8,128)(2,1)} async-done(((bf16[512,1024]{1,0:T(8,128)(2,1)}), bf16[32,1024]{1,0:T(8,128)(2,1)}) %reduce-scatter.37.cloned.1.call-update) | async-done | bytes 65552 | tf_op jit(solution)/shard_map/reduce_scatter | solution.py:313
  1387.1 58.5 %reduce-scatter.29.cloned.1.call-done = bf16[32,1024]{1,0:T(8,128)(2,1)} async-done(((bf16[512,1024]{1,0:T(8,128)(2,1)}), bf16[32,1024]{1,0:T(8,128)(2,1)}) %reduce-scatter.29.cloned.1.call-update) | async-done | bytes 65552 | tf_op jit(solution)/shard_map/reduce_scatter | solution.py:307
  1447.0 58.9 %reduce-scatter.33.cloned.1.call-done = bf16[32,1024]{1,0:T(8,128)(2,1)} async-done(((bf16[512,1024]{1,0:T(8,128)(2,1)}), bf16[32,1024]{1,0:T(8,128)(2,1)}) %reduce-scatter.33.cloned.1.call-update) | async-done | bytes 65552 | tf_op jit(solution)/shard_map/reduce_scatter | solution.py:310
  1507.4 62.7 %reduce-scatter.57.cloned.1.call-done = bf16[32,2048]{1,0:T(8,128)(2,1)} async-done(((bf16[512,2048]{1,0:T(8,128)(2,1)}), bf16[32,2048]{1,0:T(8,128)(2,1)}) %reduce-scatter.57.cloned.1.call-update) | async-done | bytes 131088 | tf_op jit(solution)/shard_map/reduce_scatter | solution.py:328
  1571.8 63.1 %reduce-scatter.53.cloned.1.call-done = bf16[32,2048]{1,0:T(8,128)(2,1)} async-done(((bf16[512,2048]{1,0:T(8,128)(2,1)}), bf16[32,2048]{1,0:T(8,128)(2,1)}) %reduce-scatter.53.cloned.1.call-update) | async-done | bytes 131088 | tf_op jit(solution)/shard_map/reduce_scatter | solution.py:325
  1636.5 73.8 %reduce-scatter.45.cloned.1.call-done = bf16[32,4096]{1,0:T(8,128)(2,1)} async-done(((bf16[512,4096]{1,0:T(8,128)(2,1)}), bf16[32,4096]{1,0:T(8,128)(2,1)}) %reduce-scatter.45.cloned.1.call-update) | async-done | bytes 262160 | tf_op jit(solution)/shard_map/reduce_scatter | solution.py:319
  1712.1 73.8 %reduce-scatter.49.cloned.1.call-done = bf16[128,1024]{1,0:T(8,128)(2,1)} async-done(((bf16[2048,1024]{1,0:T(8,128)(2,1)}), bf16[128,1024]{1,0:T(8,128)(2,1)}) %reduce-scatter.49.cloned.1.call-update) | async-done | bytes 262160 | tf_op jit(solution)/shard_map/reduce_scatter | solution.py:322
  (184 shorter events, 52.9 us)
Async XLA Ops:
  7.2 6.8 copy-start
  7.2 5.7 copy-start.4
  7.2 56.3 %all-gather.13.cloned.1.call-start = ((), (), s32[]{:S(2)}) async-start(), calls=%async_computation.20 | async-start | bytes 4456448 | tf_op jit(solution)/shard_map/all_gather | solution.py:72
  7.9 97.6 %all-gather.19.cloned.1.call-start = ((), (), s32[]{:S(2)}) async-start(), calls=%async_computation.23 | async-start | bytes 2228224 | tf_op jit(solution)/shard_map/all_gather | solution.py:67
  8.7 139.3 %all-gather.15.cloned.1.call-start = ((), (), s32[]{:S(2)}) async-start(), calls=%async_computation.21 | async-start | bytes 2228224 | tf_op jit(solution)/shard_map/all_gather | solution.py:68
  9.4 190.1 %all-gather.23.cloned.1.call-start = ((), (), s32[]{:S(2)}) async-start(), calls=%async_computation.25 | async-start | bytes 4456448 | tf_op jit(solution)/shard_map/all_gather | solution.py:73
  10.0 231.5 %all-gather.17.cloned.1.call-start = ((), (), s32[]{:S(2)}) async-start(), calls=%async_computation.22 | async-start | bytes 2228224 | tf_op jit(solution)/shard_map/all_gather | solution.py:66
  10.6 270.7 %all-gather.31.cloned.1.call-start = ((), (), s32[]{:S(2)}) async-start(), calls=%async_computation.48 | async-start | bytes 3932160 | tf_op jit(solution)/shard_map/all_gather | solution.py:109
  12.9 228.6 %copy-start.17 = (f32[640]{0:T(1024)}, f32[640]{0:T(1024)S(1)}, u32[]{:S(2)}) copy-start(f32[640]{0:T(1024)S(1)} %broadcast_multiply_fusion.1) | copy-start | bytes 7684
  13.3 0.6 copy-start.25
  13.9 227.5 %copy-start.21 = (f32[640]{0:T(1024)}, f32[640]{0:T(1024)S(1)}, u32[]{:S(2)}) copy-start(f32[640]{0:T(1024)S(1)} %fusion.77) | copy-start | bytes 7684
  14.1 185.4 %copy-start.23 = (f32[1,1024]{1,0:T(1,128)}, f32[1,1024]{1,0:T(1,128)S(1)}, u32[]{:S(2)}) copy-start(f32[1,1024]{1,0:T(1,128)S(1)} %fusion.79) | copy-start | bytes 12292
  67.4 174.1 %copy-start.19 = (f32[1,1024]{1,0:T(1,128)}, f32[1,1024]{1,0:T(1,128)S(1)}, u32[]{:S(2)}) copy-start(f32[1,1024]{1,0:T(1,128)S(1)} %get-tuple-element.87) | copy-start | bytes 12292
  67.4 174.0 %copy-start.27 = (f32[1,1024]{1,0:T(1,128)}, f32[1,1024]{1,0:T(1,128)S(1)}, u32[]{:S(2)}) copy-start(f32[1,1024]{1,0:T(1,128)S(1)} %get-tuple-element.88) | copy-start | bytes 12292
  109.8 214.4 %all-gather.29.cloned.1.call-start = ((), (), s32[]{:S(2)}) async-start(), calls=%async_computation.47 | async-start | bytes 3932160 | tf_op jit(solution)/shard_map/all_gather | solution.py:110
  152.2 213.9 %all-gather.21.cloned.1.call-start = ((), (), s32[]{:S(2)}) async-start(), calls=%async_computation.24 | async-start | bytes 2228224 | tf_op jit(solution)/shard_map/all_gather | solution.py:69
  153.0 289.0 %all-gather.25.cloned.1.call-start = ((), (), s32[]{:S(2)}) async-start(), calls=%async_computation.26 | async-start | bytes 8912896 | tf_op jit(solution)/shard_map/all_gather | solution.py:70
  153.7 363.5 %all-gather.27.cloned.1.call-start = ((), (), s32[]{:S(2)}) async-start(), calls=%async_computation.27 | async-start | bytes 8912896 | tf_op jit(solution)/shard_map/all_gather | solution.py:71
  154.3 550.0 %reduce-scatter.23.cloned.1.call-start = ((), (), s32[]{:S(2)}) async-start(), calls=%async_computation.28 | async-start | bytes 3932160 | tf_op jit(solution)/shard_map/reduce_scatter | solution.py:225
  284.2 23.1 %copy-start.2 = (bf16[1280,1024]{0,1:T(8,128)(2,1)}, bf16[1280,1024]{0,1:T(8,128)(2,1)S(1)}, u32[]{:S(2)}) copy-start(bf16[1280,1024]{0,1:T(8,128)(2,1)S(1)} %copy.60) | copy-start | bytes 7864324
  328.6 37.5 %copy-start.5 = (bf16[1,640,1024]{2,1,0:T(8,128)(2,1)S(1)}, bf16[1,640,1024]{2,1,0:T(8,128)(2,1)}, u32[]{:S(2)}) copy-start(bf16[1,640,1024]{2,1,0:T(8,128)(2,1)} %param.13) | copy-start | bytes 3932164
  348.8 20.6 %copy-start.32 = (bf16[16,64,640]{2,1,0:T(8,128)(2,1)}, bf16[16,64,640]{2,1,0:T(8,128)(2,1)S(1)}, u32[]{:S(2)}) copy-start(bf16[16,64,640]{2,1,0:T(8,128)(2,1)S(1)} %fusion.50) | copy-start | bytes 3932164
  369.3 1.5 copy-start.6
  442.0 75.2 %copy-start.12 = (bf16[1,640,1024]{2,1,0:T(8,128)(2,1)S(1)}, bf16[1,640,1024]{2,1,0:T(8,128)(2,1)}, u32[]{:S(2)}) copy-start(bf16[1,640,1024]{2,1,0:T(8,128)(2,1)} %param.14) | copy-start | bytes 3932164
  533.9 10.3 copy-start.7
  547.2 1.5 copy-start.9
  547.2 2.8 copy-start.30
  548.6 1.0 copy-start.16
  591.0 42.2 %copy-start.10 = (bf16[640,1024]{0,1:T(8,128)(2,1)S(1)}, bf16[640,1024]{0,1:T(8,128)(2,1)}, u32[]{:S(2)}) copy-start(bf16[640,1024]{0,1:T(8,128)(2,1)} %copy.59) | copy-start | bytes 3932164
  652.4 75.8 %reduce-scatter.25.cloned.1.call-start = ((), (), s32[]{:S(2)}) async-start(), calls=%async_computation.29 | async-start | bytes 3932160 | tf_op jit(solution)/shard_map/reduce_scatter | solution.py:228
  678.4 5.8 copy-start.3
  678.4 168.8 %reduce-scatter.59.cloned.1.call-start = ((), (), s32[]{:S(2)}) async-start(), calls=%async_computation.46 | async-start | bytes 24576 | tf_op jit(solution)/shard_map/reduce_scatter | solution.py:292
  699.0 5.2 copy-start.29
  704.2 23.9 %copy-start.18 = (f32[640]{0:T(1024)S(1)}, f32[640]{0:T(1024)}, u32[]{:S(2)}) copy-start(f32[640]{0:T(1024)} %copy-done.17) | copy-start | bytes 7684
  704.2 23.9 %copy-start.20 = (f32[1,1024]{1,0:T(1,128)S(1)}, f32[1,1024]{1,0:T(1,128)}, u32[]{:S(2)}) copy-start(f32[1,1024]{1,0:T(1,128)} %copy-done.19) | copy-start | bytes 12292
  708.7 25.4 %copy-start.26 = (f32[640]{0:T(1024)S(1)}, f32[640]{0:T(1024)}, u32[]{:S(2)}) copy-start(f32[640]{0:T(1024)} %copy-done.25) | copy-start | bytes 7684
  734.0 0.7 copy-start.22
  743.7 105.1 %reduce-scatter.39.cloned.1.call-start = ((), (), s32[]{:S(2)}) async-start(), calls=%async_computation.36 | async-start | bytes 3145728 | tf_op jit(solution)/shard_map/reduce_scatter | solution.py:277
  747.6 1.6 copy-start.28
  749.2 100.3 %reduce-scatter.35.cloned.1.call-start = ((), (), s32[]{:S(2)}) async-start(), calls=%async_computation.34 | async-start | bytes 3145728 | tf_op jit(solution)/shard_map/reduce_scatter | solution.py:274
  753.8 1.8 copy-start.15
  757.4 1.8 copy-start.14
  758.9 96.6 %reduce-scatter.27.cloned.1.call-start = ((), (), s32[]{:S(2)}) async-start(), calls=%async_computation.30 | async-start | bytes 3145728 | tf_op jit(solution)/shard_map/reduce_scatter | solution.py:268
  761.1 2.2 copy-start.31
  762.6 127.0 %reduce-scatter.31.cloned.1.call-start = ((), (), s32[]{:S(2)}) async-start(), calls=%async_computation.32 | async-start | bytes 3145728 | tf_op jit(solution)/shard_map/reduce_scatter | solution.py:271
  765.1 1.6 copy-start.24
  766.7 179.4 %reduce-scatter.55.cloned.1.call-start = ((), (), s32[]{:S(2)}) async-start(), calls=%async_computation.44 | async-start | bytes 6291456 | tf_op jit(solution)/shard_map/reduce_scatter | solution.py:289
  773.3 1.3 copy-start.11
  773.3 229.5 %reduce-scatter.51.cloned.1.call-start = ((), (), s32[]{:S(2)}) async-start(), calls=%async_computation.42 | async-start | bytes 6291456 | tf_op jit(solution)/shard_map/reduce_scatter | solution.py:286
  774.1 330.2 %reduce-scatter.43.cloned.1.call-start = ((), (), s32[]{:S(2)}) async-start(), calls=%async_computation.38 | async-start | bytes 12582912 | tf_op jit(solution)/shard_map/reduce_scatter | solution.py:280
  794.7 411.2 %reduce-scatter.47.cloned.1.call-start = ((), (), s32[]{:S(2)}) async-start(), calls=%async_computation.40 | async-start | bytes 12582912 | tf_op jit(solution)/shard_map/reduce_scatter | solution.py:283
  819.4 7.9 copy-start.13
  847.1 417.9 %reduce-scatter.61.cloned.1.call-start = ((), (), s32[]{:S(2)}) async-start(), calls=%async_computation.49 | async-start | bytes 139264
  848.7 476.4 %reduce-scatter.41.cloned.1.call-start = ((), (), s32[]{:S(2)}) async-start(), calls=%async_computation.37 | async-start | bytes 1114112 | tf_op jit(solution)/shard_map/reduce_scatter | solution.py:316
  849.5 536.1 %reduce-scatter.37.cloned.1.call-start = ((), (), s32[]{:S(2)}) async-start(), calls=%async_computation.35 | async-start | bytes 1114112 | tf_op jit(solution)/shard_map/reduce_scatter | solution.py:313
  850.0 595.5 %reduce-scatter.29.cloned.1.call-start = ((), (), s32[]{:S(2)}) async-start(), calls=%async_computation.31 | async-start | bytes 1114112 | tf_op jit(solution)/shard_map/reduce_scatter | solution.py:307
  855.6 650.3 %reduce-scatter.33.cloned.1.call-start = ((), (), s32[]{:S(2)}) async-start(), calls=%async_computation.33 | async-start | bytes 1114112 | tf_op jit(solution)/shard_map/reduce_scatter | solution.py:310
  889.6 680.5 %reduce-scatter.57.cloned.1.call-start = ((), (), s32[]{:S(2)}) async-start(), calls=%async_computation.45 | async-start | bytes 2228224 | tf_op jit(solution)/shard_map/reduce_scatter | solution.py:328
  946.1 688.8 %reduce-scatter.53.cloned.1.call-start = ((), (), s32[]{:S(2)}) async-start(), calls=%async_computation.43 | async-start | bytes 2228224 | tf_op jit(solution)/shard_map/reduce_scatter | solution.py:325
  1002.9 707.5 %reduce-scatter.45.cloned.1.call-start = ((), (), s32[]{:S(2)}) async-start(), calls=%async_computation.39 | async-start | bytes 4456448 | tf_op jit(solution)/shard_map/reduce_scatter | solution.py:319
  1104.3 101.7 %copy-start.8 = (f32[1,640,1024]{2,1,0:T(8,128)S(1)}, f32[1,640,1024]{2,1,0:T(8,128)}, u32[]{:S(2)}) copy-start(f32[1,640,1024]{2,1,0:T(8,128)} %copy-done.6) | copy-start | bytes 7864324
  1104.3 681.6 %reduce-scatter.49.cloned.1.call-start = ((), (), s32[]{:S(2)}) async-start(), calls=%async_computation.41 | async-start | bytes 4456448 | tf_op jit(solution)/shard_map/reduce_scatter | solution.py:322
  1206.0 581.7 %copy-start.1 = (bf16[8,1024]{1,0:T(8,128)(2,1)S(1)}, bf16[8,1024]{1,0:T(8,128)(2,1)}, u32[]{:S(2)}) copy-start(bf16[8,1024]{1,0:T(8,128)(2,1)} %param.17) | copy-start | bytes 49156
Sparse Core Ops, SparseCore 0:
  10.2 53.2 all-gather.12
  65.7 39.8 all-gather.18
  107.7 40.1 all-gather.14
  150.0 49.4 all-gather.22
  201.5 39.9 all-gather.16
  243.4 37.7 all-gather.30
  283.4 39.0 all-gather.28
  324.6 41.4 all-gather.20
  368.3 73.6 all-gather.24
  444.0 73.1 all-gather.26
  652.5 35.8 reduce-scatter.22
  690.5 37.5 reduce-scatter.24
  743.8 9.7 reduce-scatter.58
  755.7 31.8 reduce-scatter.38
  789.7 31.8 reduce-scatter.34
  823.7 31.8 reduce-scatter.26
  857.7 31.8 reduce-scatter.30
  891.8 54.2 reduce-scatter.54
  948.5 54.3 reduce-scatter.50
  1005.0 99.2 reduce-scatter.42
  1106.7 99.2 reduce-scatter.46
  1210.0 55.0 reduce-scatter.60
  1268.7 56.3 reduce-scatter.40
  1329.0 56.4 reduce-scatter.36
  1389.2 56.3 reduce-scatter.28
  1449.5 56.4 reduce-scatter.32
  1509.5 60.5 reduce-scatter.56
  1574.3 60.5 reduce-scatter.52
  1638.8 71.5 reduce-scatter.44
  1714.5 71.3 reduce-scatter.48
where the time goes:
time: 1800 us; the launch traced here: 1790 us
  waiting for transfers between devices  1310 us (73%)
  matrix products  288 us (16%)
  other arithmetic  117 us (6%)
  local copies, waits for them, and re-layouts  60.6 us (3%)
    reduce_scatter x1, waiting for transfers between devices, shards(): lax.psum_scatter(part_down.astype(jnp.bfloat16), 'seq', scatter_dimension...  101 us
    reduce_scatter x1, waiting for transfers between devices, shards(): lax.psum_scatter(part_up.astype(jnp.bfloat16), 'seq', scatter_dimension=0...  101 us
    reduce_scatter x1, waiting for transfers between devices, shards(): lax.psum_scatter(seq_up.astype(jnp.bfloat16), 'items', scatter_dimension=...  73.8 us
    reduce_scatter x1, waiting for transfers between devices, shards(): lax.psum_scatter(seq_down.astype(jnp.bfloat16), 'items', scatter_dimensio...  73.8 us
    all_gather x1, waiting for transfers between devices, shards(): lax.all_gather(w_up, 'items', axis=0, tiled=True)  70.7 us
    reduce_scatter x1, waiting for transfers between devices, shards(): lax.psum_scatter(seq_ada_one.astype(jnp.bfloat16), 'items', scatter_dimen...  63.1 us
    reduce_scatter x1, waiting for transfers between devices, shards(): lax.psum_scatter(seq_ada_two.astype(jnp.bfloat16), 'items', scatter_dimen...  62.7 us
    reduce_scatter x1, waiting for transfers between devices, shards(): lax.psum_scatter(seq_value.astype(jnp.bfloat16), 'items', scatter_dimensi...  58.9 us
  transfers between devices with their start and end apart: 30, of which 25 were waited for; matrix products, arithmetic and copies ran while one was open for 17% of the time, Pallas kernels for 0%

commit v1 on v0

--- a/solution.py
+++ b/solution.py
@@ -4,12 +4,22 @@
 import jax.numpy as jnp
 from jax import lax
 from jax.sharding import PartitionSpec as P
+from jax.lax import all_to_all, axis_size
 
 HEADS = 16
 HEAD_DIM = 64
 PROMPT = 640
 EPSILON = 1e-05
 MASKED = -1e30
+bring_rails_for = lambda buf, array_dim: jnp.concatenate(
+    all_to_all(
+        jnp.stack([buf for _ in range(axis_size("items"))], 0),
+        axis_name="items",
+        split_axis=0,
+        concat_axis=0,
+    ),
+    array_dim,
+)
 
 
 def exact(left, right):
@@ -67,7 +77,7 @@
         lax.all_gather(w_key, "items", axis=0, tiled=True),
         lax.all_gather(w_value, "items", axis=0, tiled=True),
         lax.all_gather(w_out, "items", axis=0, tiled=True),
-        lax.all_gather(w_up, "items", axis=0, tiled=True),
+        bring_rails_for(w_up, 0),
         lax.all_gather(w_down, "items", axis=0, tiled=True),
         lax.all_gather(w_ada_one, "items", axis=0, tiled=True),
         lax.all_gather(w_ada_two, "items", axis=0, tiled=True),

time: 1800 us -> 1840 us (1.022)
  waiting for transfers between devices: 1310 us -> 1350 us
    all_gather x1, waiting for transfers between devices: 38 us -> 127 us  [shards(): lax.all_gather(w_query, 'items', axis=0, tiled=True)]
    all_gather x1 -> x0, waiting for transfers between devices: 70.7 us -> none  [shards(): lax.all_gather(w_up, 'items', axis=0, tiled=True)]
    all_gather x1, waiting for transfers between devices: 0.02 us -> 38.2 us  [shards(): lax.all_gather(values_here, 'seq', axis=1, tiled=True)]
    all_gather x1, waiting for transfers between devices: 42.8 us -> 18.4 us  [shards(): lax.all_gather(w_down, 'items', axis=0, tiled=True)]
    all_gather x1, waiting for transfers between devices: 43.8 us -> 64.1 us  [shards(): lax.all_gather(w_ada_two, 'items', axis=0, tiled=True)]
    unnamed x31 -> x30, waiting for transfers between devices: 53.1 us -> 52.6 us
  transfers between devices with their start and end apart: 30 -> 30, of which waited for: 25 -> 24; matrix products, arithmetic and copies ran while one was open for 17% -> 17% of each run, Pallas kernels for 0% -> 0%
where the time goes in v1:
time: 1840 us
  waiting for transfers between devices  1350 us (73%)
  matrix products  286 us (16%)
  other arithmetic  118 us (6%)
  local copies, waits for them, and re-layouts  64.6 us (4%)
    all_gather x1, waiting for transfers between devices, shards(): lax.all_gather(w_query, 'items', axis=0, tiled=True)  127 us
    reduce_scatter x1, waiting for transfers between devices, shards(): lax.psum_scatter(part_up.astype(jnp.bfloat16), 'seq', scatter_dimension=0...  101 us
    reduce_scatter x1, waiting for transfers between devices, shards(): lax.psum_scatter(part_down.astype(jnp.bfloat16), 'seq', scatter_dimension...  101 us
    reduce_scatter x1, waiting for transfers between devices, shards(): lax.psum_scatter(seq_down.astype(jnp.bfloat16), 'items', scatter_dimensio...  74.1 us
    reduce_scatter x1, waiting for transfers between devices, shards(): lax.psum_scatter(seq_up.astype(jnp.bfloat16), 'items', scatter_dimension=...  73.8 us
    all_gather x1, waiting for transfers between devices, shards(): lax.all_gather(w_ada_two, 'items', axis=0, tiled=True)  64.1 us
    reduce_scatter x1, waiting for transfers between devices, shards(): lax.psum_scatter(seq_ada_one.astype(jnp.bfloat16), 'items', scatter_dimen...  63 us
    reduce_scatter x1, waiting for transfers between devices, shards(): lax.psum_scatter(seq_ada_two.astype(jnp.bfloat16), 'items', scatter_dimen...  62.7 us
  transfers between devices with their start and end apart: 30, of which 24 were waited for; matrix products, arithmetic and copies ran while one was open for 17% of the time, Pallas kernels for 0%

profile of v1, /device:TPU:0, one launch (start us, length us, event | category | flops | bytes accessed | tf_op | source)
XLA Modules:
  0.0 1838.2 jit_solution(10187829405015419222)
XLA Ops:
  13.5 50.0 %all-gather.12.cloned.1.call-done = bf16[1024,2048]{1,0:T(8,128)(2,1)} async-done(((bf16[64,2048]{1,0:T(8,128)(2,1)}), bf16[1024,2048]{1,0:T(8,128)(2,1)}) %all-gather.12.cloned.1.call-update) | async-done | bytes 4194320 | tf_op jit(solution)/shard_map/all_gather | solution.py:82
  63.5 3.9 fusion.75
  67.4 38.1 %all-gather.18.cloned.1.call-done = bf16[1024,1024]{1,0:T(8,128)(2,1)} async-done(((bf16[64,1024]{1,0:T(8,128)(2,1)}), bf16[1024,1024]{1,0:T(8,128)(2,1)}) %all-gather.18.cloned.1.call-update) | async-done | bytes 2097168 | tf_op jit(solution)/shard_map/all_gather | solution.py:77
  105.6 4.2 convolution_convert_fusion.1
  109.9 38.1 %all-gather.14.cloned.1.call-done = bf16[1024,1024]{1,0:T(8,128)(2,1)} async-done(((bf16[64,1024]{1,0:T(8,128)(2,1)}), bf16[1024,1024]{1,0:T(8,128)(2,1)}) %all-gather.14.cloned.1.call-update) | async-done | bytes 2097168 | tf_op jit(solution)/shard_map/all_gather | solution.py:78
  148.0 4.2 convolution_convert_fusion.3
  153.0 4.3 stack.2
  157.3 4.7 all-to-all-start
  164.2 126.6 %all-gather.16.cloned.1.call-done = bf16[1024,1024]{1,0:T(8,128)(2,1)} async-done(((bf16[64,1024]{1,0:T(8,128)(2,1)}), bf16[1024,1024]{1,0:T(8,128)(2,1)}) %all-gather.16.cloned.1.call-update) | async-done | bytes 2097168 | tf_op jit(solution)/shard_map/all_gather | solution.py:76
  290.8 3.2 convolution_convert_fusion.2
  295.4 64.1 %all-gather.22.cloned.1.call-done = bf16[1024,2048]{1,0:T(8,128)(2,1)} async-done(((bf16[64,2048]{1,0:T(8,128)(2,1)}), bf16[1024,2048]{1,0:T(8,128)(2,1)}) %all-gather.22.cloned.1.call-update) | async-done | bytes 4194320 | tf_op jit(solution)/shard_map/all_gather | solution.py:83
  359.5 3.9 fusion.73
  363.4 36.5 %all-gather.28.cloned.1.call-done = bf16[1280,1024]{1,0:T(8,128)(2,1)} async-done(((bf16[640,1024]{1,0:T(8,128)(2,1)}), bf16[1280,1024]{1,0:T(8,128)(2,1)}) %all-gather.28.cloned.1.call-update) | async-done | bytes 2621456 | tf_op jit(solution)/shard_map/all_gather | solution.py:119
  400.0 3.0 copy.60
  403.0 38.2 %all-gather.26.cloned.1.call-done = bf16[1280,1024]{1,0:T(8,128)(2,1)} async-done(((bf16[640,1024]{1,0:T(8,128)(2,1)}), bf16[1280,1024]{1,0:T(8,128)(2,1)}) %all-gather.26.cloned.1.call-update) | async-done | bytes 2621456 | tf_op jit(solution)/shard_map/all_gather | solution.py:120
  441.1 4.4 copy.58
  445.5 21.7 %fusion.93 = (f32[16,640]{1,0:T(8,128)S(1)}, f32[16,640,1280]{2,1,0:T(8,128)}) fusion(bf16[640,16,64]{0,2,1:T(8,128)(2,1)} %bitcast.285, bf16[1280,16,64]{0,2,1:T(8,128)(2,1)S(1)} %bitcast.279, pred[640,1280]{1,0:T(8,128)(4,1)S(1)} %and_or_fusion), kind=kOutput, calls=%fused_computation.153 | convolution fusion | flops 1717032960 | bytes 57221120 | tf_op jit(solution)/shard_map/while/body/eval_jaxpr/qhd,khd->hqk/dot_general | solution.py:125
  467.2 17.5 fusion
  484.7 19.4 %fusion.50 = bf16[16,64,640]{2,1,0:T(8,128)(2,1)S(1)} fusion(bf16[1280,16,64]{0,2,1:T(8,128)(2,1)S(1)} %bitcast.291, f32[16,640,1280]{2,1,0:T(8,128)} %get-tuple-element.90, f32[16,640]{1,0:T(8,128)S(1)} %fusion, f32[16,640]{1,0:T(8,128)S(1)} %get-tuple-element.89), kind=kOutput, calls=%fused_computation.97 | convolution fusion | flops 1717698560 | bytes 56442880 | tf_op jit(solution)/shard_map/while/body/eval_jaxpr/hqk,khd->qhd/dot_general | solution.py:145
  504.2 3.7 fusion.94
  509.8 32.4 %fusion.6 = (f32[640,4096]{1,0:T(8,128)}, f32[640,4096]{1,0:T(8,128)}) fusion(bf16[1024,4096]{1,0:T(8,128)(2,1)} %bitcast.20, f32[1024]{0:T(1024)S(1)} %bitcast.331, f32[640]{0:T(1024)S(1)} %fusion.78, f32[1,640,1024]{2,1,0:T(8,128)} %copy-done.6, f32[640]{0:T(1024)S(1)} %broadcast_multiply_fusion, f32[1024]{0:T(1024)S(1)} %bitcast.311), kind=kOutput, calls=%fused_computation.13 | convolution fusion | flops 5534515200 | bytes 31994880 | tf_op jit(solution)/shard_map/dot_general | solution.py:160
  542.2 18.4 %all-gather.24.cloned.1.call-done = bf16[4096,1024]{1,0:T(8,128)(2,1)} async-done(((bf16[256,1024]{1,0:T(8,128)(2,1)}), bf16[4096,1024]{1,0:T(8,128)(2,1)}) %all-gather.24.cloned.1.call-update) | async-done | bytes 8388624 | tf_op jit(solution)/shard_map/all_gather | solution.py:81
  560.6 16.8 add_convert_fusion
  577.4 10.2 fusion.95
  587.6 2.1 fusion.46
  595.8 38.6 %multiply_reduce_fusion = (f32[16,640]{1,0:T(8,128)S(1)}, f32[16,640,1280]{2,1,0:T(8,128)}) fusion(f32[16,640,1280]{2,1,0:T(8,128)} %get-tuple-element.90, f32[16,640]{1,0:T(8,128)S(1)} %log_add_fusion, bf16[640,16,64]{0,2,1:T(8,128)(2,1)S(1)} %bitcast.288, bf16[1280,16,64]{0,2,1:T(8,128)(2,1)} %bitcast.290), kind=kOutput, calls=%fused_computation.1 | convolution fusion | flops 1717032960 | bytes 108871680 | tf_op jit(solution)/shard_map/while/body/eval_jaxpr/qhd,khd->hqk/dot_general | solution.py:189
  634.4 42.2 %multiply_convert_fusion = bf16[16,640,1280]{2,1,0:T(8,128)(2,1)} fusion(f32[16,640,1280]{2,1,0:T(8,128)} %get-tuple-element.96, f32[16,640,1280]{2,1,0:T(8,128)} %get-tuple-element.90, f32[16,640]{1,0:T(8,128)S(1)} %get-tuple-element.95, f32[16,640]{1,0:T(8,128)S(1)} %log_add_fusion), kind=kLoop, calls=%fused_computation | loop fusion | flops 52428800 | bytes 131153920 | tf_op jit(solution)/shard_map/while/body/eval_jaxpr/convert_element_type | solution.py:193
  676.6 14.6 multiply_convert_fusion.5
  691.2 4.5 copy.62
  695.8 21.4 %fusion.36 = bf16[16,64,1280]{2,1,0:T(8,128)(2,1)} fusion(bf16[640,16,64]{0,2,1:T(8,128)(2,1)S(1)} %bitcast.289, f32[16,640,1280]{2,1,0:T(8,128)} %get-tuple-element.90, f32[16,640]{1,0:T(8,128)S(1)} %log_add_fusion), kind=kOutput, calls=%fused_computation.67 | convolution fusion | flops 1705246720 | bytes 56401920 | tf_op jit(solution)/shard_map/while/body/eval_jaxpr/hqk,qhd->khd/dot_general | solution.py:219
  717.2 4.5 copy.63
  721.9 5.7 fusion.69
  727.6 14.9 multiply_convert_fusion.6
  742.4 5.2 fusion.96
  747.6 4.4 fusion.56
  752.0 19.7 %reduce-scatter.25.cloned.1.call-done = bf16[1,640,1024]{2,1,0:T(8,128)(2,1)} async-done(((bf16[1,1280,1024]{2,1,0:T(8,128)(2,1)}), bf16[1,640,1024]{2,1,0:T(8,128)(2,1)}) %reduce-scatter.25.cloned.1.call-update) | async-done | bytes 1310736 | tf_op jit(solution)/shard_map/reduce_scatter | solution.py:238
  771.7 5.9 fusion.45
  778.3 2.5 fusion.43
  780.7 5.5 fusion.71
  787.7 3.5 convert_bitcast_fusion.2
  792.8 4.5 fusion.90
  810.4 6.5 multiply_convert_fusion.2
  818.9 11.5 convert_bitcast_fusion.1
  830.4 7.8 copy.71
  838.3 24.6 %fusion.9 = bf16[4096,640]{0,1:T(8,128)(2,1)} fusion(f32[640,4096]{1,0:T(8,128)} %get-tuple-element.94), kind=kLoop, calls=%fused_computation.16 | loop fusion | flops 170393600 | bytes 15728640 | tf_op jit(solution)/shard_map/convert_element_type | solution.py:162
  862.9 7.9 copy.83
  870.8 11.5 convert_bitcast_fusion
  882.4 8.2 copy.73
  893.7 5.5 reduce-scatter.27.cloned.1.call-done
  899.3 34.0 %reduce-scatter.31.cloned.1.call-done = bf16[512,1024]{1,0:T(8,128)(2,1)} async-done(((bf16[1024,1024]{1,0:T(8,128)(2,1)}), bf16[512,1024]{1,0:T(8,128)(2,1)}) %reduce-scatter.31.cloned.1.call-update) | async-done | bytes 1048592 | tf_op jit(solution)/shard_map/reduce_scatter | solution.py:281
  933.4 56.4 %reduce-scatter.55.cloned.1.call-done = bf16[512,2048]{1,0:T(8,128)(2,1)} async-done(((bf16[1024,2048]{1,0:T(8,128)(2,1)}), bf16[512,2048]{1,0:T(8,128)(2,1)}) %reduce-scatter.55.cloned.1.call-update) | async-done | bytes 2097168 | tf_op jit(solution)/shard_map/reduce_scatter | solution.py:299
  989.9 56.5 %reduce-scatter.51.cloned.1.call-done = bf16[512,2048]{1,0:T(8,128)(2,1)} async-done(((bf16[1024,2048]{1,0:T(8,128)(2,1)}), bf16[512,2048]{1,0:T(8,128)(2,1)}) %reduce-scatter.51.cloned.1.call-update) | async-done | bytes 2097168 | tf_op jit(solution)/shard_map/reduce_scatter | solution.py:296
  1046.4 101.5 %reduce-scatter.43.cloned.1.call-done = bf16[512,4096]{1,0:T(8,128)(2,1)} async-done(((bf16[1024,4096]{1,0:T(8,128)(2,1)}), bf16[512,4096]{1,0:T(8,128)(2,1)}) %reduce-scatter.43.cloned.1.call-update) | async-done | bytes 4194320 | tf_op jit(solution)/shard_map/reduce_scatter | solution.py:290
  1148.2 101.2 %reduce-scatter.47.cloned.1.call-done = bf16[2048,1024]{1,0:T(8,128)(2,1)} async-done(((bf16[4096,1024]{1,0:T(8,128)(2,1)}), bf16[2048,1024]{1,0:T(8,128)(2,1)}) %reduce-scatter.47.cloned.1.call-update) | async-done | bytes 4194320 | tf_op jit(solution)/shard_map/reduce_scatter | solution.py:293
  1249.5 13.2 fusion.48
  1262.6 45.9 %reduce-scatter.61.cloned.1.call-done = bf16[32,8]{1,0:T(8,128)(2,1)} async-done(((bf16[512,8]{1,0:T(8,128)(2,1)}), bf16[32,8]{1,0:T(8,128)(2,1)}) %reduce-scatter.61.cloned.1.call-update) | async-done | bytes 528
  1309.9 58.7 %reduce-scatter.41.cloned.1.call-done = bf16[32,1024]{1,0:T(8,128)(2,1)} async-done(((bf16[512,1024]{1,0:T(8,128)(2,1)}), bf16[32,1024]{1,0:T(8,128)(2,1)}) %reduce-scatter.41.cloned.1.call-update) | async-done | bytes 65552 | tf_op jit(solution)/shard_map/reduce_scatter | solution.py:326
  1370.2 59.0 %reduce-scatter.37.cloned.1.call-done = bf16[32,1024]{1,0:T(8,128)(2,1)} async-done(((bf16[512,1024]{1,0:T(8,128)(2,1)}), bf16[32,1024]{1,0:T(8,128)(2,1)}) %reduce-scatter.37.cloned.1.call-update) | async-done | bytes 65552 | tf_op jit(solution)/shard_map/reduce_scatter | solution.py:323
  1430.7 58.5 %reduce-scatter.29.cloned.1.call-done = bf16[32,1024]{1,0:T(8,128)(2,1)} async-done(((bf16[512,1024]{1,0:T(8,128)(2,1)}), bf16[32,1024]{1,0:T(8,128)(2,1)}) %reduce-scatter.29.cloned.1.call-update) | async-done | bytes 65552 | tf_op jit(solution)/shard_map/reduce_scatter | solution.py:317
  1490.7 59.0 %reduce-scatter.33.cloned.1.call-done = bf16[32,1024]{1,0:T(8,128)(2,1)} async-done(((bf16[512,1024]{1,0:T(8,128)(2,1)}), bf16[32,1024]{1,0:T(8,128)(2,1)}) %reduce-scatter.33.cloned.1.call-update) | async-done | bytes 65552 | tf_op jit(solution)/shard_map/reduce_scatter | solution.py:320
  1551.2 62.7 %reduce-scatter.57.cloned.1.call-done = bf16[32,2048]{1,0:T(8,128)(2,1)} async-done(((bf16[512,2048]{1,0:T(8,128)(2,1)}), bf16[32,2048]{1,0:T(8,128)(2,1)}) %reduce-scatter.57.cloned.1.call-update) | async-done | bytes 131088 | tf_op jit(solution)/shard_map/reduce_scatter | solution.py:338
  1615.5 63.0 %reduce-scatter.53.cloned.1.call-done = bf16[32,2048]{1,0:T(8,128)(2,1)} async-done(((bf16[512,2048]{1,0:T(8,128)(2,1)}), bf16[32,2048]{1,0:T(8,128)(2,1)}) %reduce-scatter.53.cloned.1.call-update) | async-done | bytes 131088 | tf_op jit(solution)/shard_map/reduce_scatter | solution.py:335
  1680.1 73.8 %reduce-scatter.45.cloned.1.call-done = bf16[32,4096]{1,0:T(8,128)(2,1)} async-done(((bf16[512,4096]{1,0:T(8,128)(2,1)}), bf16[32,4096]{1,0:T(8,128)(2,1)}) %reduce-scatter.45.cloned.1.call-update) | async-done | bytes 262160 | tf_op jit(solution)/shard_map/reduce_scatter | solution.py:329
  1755.6 74.1 %reduce-scatter.49.cloned.1.call-done = bf16[128,1024]{1,0:T(8,128)(2,1)} async-done(((bf16[2048,1024]{1,0:T(8,128)(2,1)}), bf16[128,1024]{1,0:T(8,128)(2,1)}) %reduce-scatter.49.cloned.1.call-update) | async-done | bytes 262160 | tf_op jit(solution)/shard_map/reduce_scatter | solution.py:332
  (188 shorter events, 53.8 us)
Async XLA Ops:
  7.2 6.2 copy-start
  7.2 5.7 copy-start.4
  7.2 56.3 %all-gather.12.cloned.1.call-start = ((), (), s32[]{:S(2)}) async-start(), calls=%async_computation.21 | async-start | bytes 4456448 | tf_op jit(solution)/shard_map/all_gather | solution.py:82
  7.9 97.6 %all-gather.18.cloned.1.call-start = ((), (), s32[]{:S(2)}) async-start(), calls=%async_computation.24 | async-start | bytes 2228224 | tf_op jit(solution)/shard_map/all_gather | solution.py:77
  8.7 139.3 %all-gather.14.cloned.1.call-start = ((), (), s32[]{:S(2)}) async-start(), calls=%async_computation.22 | async-start | bytes 2228224 | tf_op jit(solution)/shard_map/all_gather | solution.py:78
  9.4 281.3 %all-gather.16.cloned.1.call-start = ((), (), s32[]{:S(2)}) async-start(), calls=%async_computation.23 | async-start | bytes 2228224 | tf_op jit(solution)/shard_map/all_gather | solution.py:76
  10.0 349.5 %all-gather.22.cloned.1.call-start = ((), (), s32[]{:S(2)}) async-start(), calls=%async_computation.26 | async-start | bytes 4456448 | tf_op jit(solution)/shard_map/all_gather | solution.py:83
  10.6 389.4 %all-gather.28.cloned.1.call-start = ((), (), s32[]{:S(2)}) async-start(), calls=%async_computation.48 | async-start | bytes 3932160 | tf_op jit(solution)/shard_map/all_gather | solution.py:119
  12.9 277.9 %copy-start.19 = (f32[640]{0:T(1024)}, f32[640]{0:T(1024)S(1)}, u32[]{:S(2)}) copy-start(f32[640]{0:T(1024)S(1)} %broadcast_multiply_fusion.1) | copy-start | bytes 7684
  13.3 96.5 %copy-start.27 = (f32[640]{0:T(1024)}, f32[640]{0:T(1024)S(1)}, u32[]{:S(2)}) copy-start(f32[640]{0:T(1024)S(1)} %fusion.44) | copy-start | bytes 7684
  13.4 277.4 %copy-start.23 = (f32[640]{0:T(1024)}, f32[640]{0:T(1024)S(1)}, u32[]{:S(2)}) copy-start(f32[640]{0:T(1024)S(1)} %fusion.77) | copy-start | bytes 7684
  13.5 346.0 %copy-start.25 = (f32[1,1024]{1,0:T(1,128)}, f32[1,1024]{1,0:T(1,128)S(1)}, u32[]{:S(2)}) copy-start(f32[1,1024]{1,0:T(1,128)S(1)} %fusion.79) | copy-start | bytes 12292
  67.4 223.3 %copy-start.21 = (f32[1,1024]{1,0:T(1,128)}, f32[1,1024]{1,0:T(1,128)S(1)}, u32[]{:S(2)}) copy-start(f32[1,1024]{1,0:T(1,128)S(1)} %get-tuple-element.87) | copy-start | bytes 12292
  67.4 223.3 %copy-start.29 = (f32[1,1024]{1,0:T(1,128)}, f32[1,1024]{1,0:T(1,128)S(1)}, u32[]{:S(2)}) copy-start(f32[1,1024]{1,0:T(1,128)S(1)} %get-tuple-element.88) | copy-start | bytes 12292
  109.8 43.1 %copy-start.18 = (bf16[64,4096]{1,0:T(8,128)(2,1)S(1)}, bf16[64,4096]{1,0:T(8,128)(2,1)}, u32[]{:S(2)}) copy-start(bf16[64,4096]{1,0:T(8,128)(2,1)} %param.22) | copy-start | bytes 1572868
  109.8 331.3 %all-gather.26.cloned.1.call-start = ((), (), s32[]{:S(2)}) async-start(), calls=%async_computation.47 | async-start | bytes 3932160 | tf_op jit(solution)/shard_map/all_gather | solution.py:120
  152.2 352.0 %all-gather.20.cloned.1.call-start = ((), (), s32[]{:S(2)}) async-start(), calls=%async_computation.25 | async-start | bytes 2228224 | tf_op jit(solution)/shard_map/all_gather | solution.py:79
  157.3 352.5 %all-to-all-start = ((bf16[16,64,4096]{2,1,0:T(8,128)(2,1)}), bf16[16,64,4096]{2,1,0:T(8,128)(2,1)}, u32[]{:S(2)}, u32[]{:S(2)}) async-start(bf16[16,64,4096]{2,1,0:T(8,128)(2,1)} %stack.2), calls=%async_computation | async-start | bytes 16777216 | tf_op jit(solution)/shard_map/all_to_all | solution.py:15
  162.0 398.6 %all-gather.24.cloned.1.call-start = ((), (), s32[]{:S(2)}) async-start(), calls=%async_computation.27 | async-start | bytes 8912896 | tf_op jit(solution)/shard_map/all_gather | solution.py:81
  162.7 584.9 %reduce-scatter.23.cloned.1.call-start = ((), (), s32[]{:S(2)}) async-start(), calls=%async_computation.28 | async-start | bytes 3932160 | tf_op jit(solution)/shard_map/reduce_scatter | solution.py:235
  402.9 42.6 %copy-start.2 = (bf16[1280,1024]{0,1:T(8,128)(2,1)}, bf16[1280,1024]{0,1:T(8,128)(2,1)S(1)}, u32[]{:S(2)}) copy-start(bf16[1280,1024]{0,1:T(8,128)(2,1)S(1)} %copy.60) | copy-start | bytes 7864324
  467.2 17.5 copy-start.11
  484.7 19.4 %copy-start.5 = (bf16[1,640,1024]{2,1,0:T(8,128)(2,1)S(1)}, bf16[1,640,1024]{2,1,0:T(8,128)(2,1)}, u32[]{:S(2)}) copy-start(bf16[1,640,1024]{2,1,0:T(8,128)(2,1)} %param.13) | copy-start | bytes 3932164
  504.1 3.7 copy-start.34
  507.9 1.5 copy-start.6
  509.8 50.8 %copy-start.13 = (bf16[1,640,1024]{2,1,0:T(8,128)(2,1)S(1)}, bf16[1,640,1024]{2,1,0:T(8,128)(2,1)}, u32[]{:S(2)}) copy-start(bf16[1,640,1024]{2,1,0:T(8,128)(2,1)} %param.14) | copy-start | bytes 3932164
  577.4 10.2 copy-start.7
  590.7 1.5 copy-start.9
  590.7 2.8 copy-start.32
  592.1 1.1 copy-start.17
  634.4 42.2 %copy-start.10 = (bf16[640,1024]{0,1:T(8,128)(2,1)S(1)}, bf16[640,1024]{0,1:T(8,128)(2,1)}, u32[]{:S(2)}) copy-start(bf16[640,1024]{0,1:T(8,128)(2,1)} %copy.59) | copy-start | bytes 3932164
  695.8 76.0 %reduce-scatter.25.cloned.1.call-start = ((), (), s32[]{:S(2)}) async-start(), calls=%async_computation.29 | async-start | bytes 3932160 | tf_op jit(solution)/shard_map/reduce_scatter | solution.py:238
  721.8 5.8 copy-start.3
  721.8 168.9 %reduce-scatter.59.cloned.1.call-start = ((), (), s32[]{:S(2)}) async-start(), calls=%async_computation.46 | async-start | bytes 24576 | tf_op jit(solution)/shard_map/reduce_scatter | solution.py:302
  742.4 5.2 copy-start.31
  747.6 24.1 %copy-start.20 = (f32[640]{0:T(1024)S(1)}, f32[640]{0:T(1024)}, u32[]{:S(2)}) copy-start(f32[640]{0:T(1024)} %copy-done.19) | copy-start | bytes 7684
  747.6 24.1 %copy-start.22 = (f32[1,1024]{1,0:T(1,128)S(1)}, f32[1,1024]{1,0:T(1,128)}, u32[]{:S(2)}) copy-start(f32[1,1024]{1,0:T(1,128)} %copy-done.21) | copy-start | bytes 12292
  752.0 25.5 %copy-start.28 = (f32[640]{0:T(1024)S(1)}, f32[640]{0:T(1024)}, u32[]{:S(2)}) copy-start(f32[640]{0:T(1024)} %copy-done.27) | copy-start | bytes 7684
  787.2 105.0 %reduce-scatter.39.cloned.1.call-start = ((), (), s32[]{:S(2)}) async-start(), calls=%async_computation.36 | async-start | bytes 3145728 | tf_op jit(solution)/shard_map/reduce_scatter | solution.py:287
  791.2 1.6 copy-start.30
  792.8 100.3 %reduce-scatter.35.cloned.1.call-start = ((), (), s32[]{:S(2)}) async-start(), calls=%async_computation.34 | async-start | bytes 3145728 | tf_op jit(solution)/shard_map/reduce_scatter | solution.py:284
  797.4 1.8 copy-start.16
  801.0 1.8 copy-start.15
  802.5 96.7 %reduce-scatter.27.cloned.1.call-start = ((), (), s32[]{:S(2)}) async-start(), calls=%async_computation.30 | async-start | bytes 3145728 | tf_op jit(solution)/shard_map/reduce_scatter | solution.py:278
  804.6 2.2 copy-start.33
  806.1 127.2 %reduce-scatter.31.cloned.1.call-start = ((), (), s32[]{:S(2)}) async-start(), calls=%async_computation.32 | async-start | bytes 3145728 | tf_op jit(solution)/shard_map/reduce_scatter | solution.py:281
  808.7 1.6 copy-start.26
  810.2 179.5 %reduce-scatter.55.cloned.1.call-start = ((), (), s32[]{:S(2)}) async-start(), calls=%async_computation.44 | async-start | bytes 6291456 | tf_op jit(solution)/shard_map/reduce_scatter | solution.py:299
  816.9 1.3 copy-start.12
  816.9 229.4 %reduce-scatter.51.cloned.1.call-start = ((), (), s32[]{:S(2)}) async-start(), calls=%async_computation.42 | async-start | bytes 6291456 | tf_op jit(solution)/shard_map/reduce_scatter | solution.py:296
  817.5 330.4 %reduce-scatter.43.cloned.1.call-start = ((), (), s32[]{:S(2)}) async-start(), calls=%async_computation.38 | async-start | bytes 12582912 | tf_op jit(solution)/shard_map/reduce_scatter | solution.py:290
  838.3 411.2 %reduce-scatter.47.cloned.1.call-start = ((), (), s32[]{:S(2)}) async-start(), calls=%async_computation.40 | async-start | bytes 12582912 | tf_op jit(solution)/shard_map/reduce_scatter | solution.py:293
  862.9 7.9 copy-start.14
  890.6 418.0 %reduce-scatter.61.cloned.1.call-start = ((), (), s32[]{:S(2)}) async-start(), calls=%async_computation.49 | async-start | bytes 139264
  892.2 476.5 %reduce-scatter.41.cloned.1.call-start = ((), (), s32[]{:S(2)}) async-start(), calls=%async_computation.37 | async-start | bytes 1114112 | tf_op jit(solution)/shard_map/reduce_scatter | solution.py:326
  892.9 536.2 %reduce-scatter.37.cloned.1.call-start = ((), (), s32[]{:S(2)}) async-start(), calls=%async_computation.35 | async-start | bytes 1114112 | tf_op jit(solution)/shard_map/reduce_scatter | solution.py:323
  893.7 595.5 %reduce-scatter.29.cloned.1.call-start = ((), (), s32[]{:S(2)}) async-start(), calls=%async_computation.31 | async-start | bytes 1114112 | tf_op jit(solution)/shard_map/reduce_scatter | solution.py:317
  899.3 650.4 %reduce-scatter.33.cloned.1.call-start = ((), (), s32[]{:S(2)}) async-start(), calls=%async_computation.33 | async-start | bytes 1114112 | tf_op jit(solution)/shard_map/reduce_scatter | solution.py:320
  933.3 680.5 %reduce-scatter.57.cloned.1.call-start = ((), (), s32[]{:S(2)}) async-start(), calls=%async_computation.45 | async-start | bytes 2228224 | tf_op jit(solution)/shard_map/reduce_scatter | solution.py:338
  989.8 688.6 %reduce-scatter.53.cloned.1.call-start = ((), (), s32[]{:S(2)}) async-start(), calls=%async_computation.43 | async-start | bytes 2228224 | tf_op jit(solution)/shard_map/reduce_scatter | solution.py:335
  1046.4 707.4 %reduce-scatter.45.cloned.1.call-start = ((), (), s32[]{:S(2)}) async-start(), calls=%async_computation.39 | async-start | bytes 4456448 | tf_op jit(solution)/shard_map/reduce_scatter | solution.py:329
  1148.0 101.5 %copy-start.8 = (f32[1,640,1024]{2,1,0:T(8,128)S(1)}, f32[1,640,1024]{2,1,0:T(8,128)}, u32[]{:S(2)}) copy-start(f32[1,640,1024]{2,1,0:T(8,128)} %copy-done.6) | copy-start | bytes 7864324
  1148.0 681.7 %reduce-scatter.49.cloned.1.call-start = ((), (), s32[]{:S(2)}) async-start(), calls=%async_computation.41 | async-start | bytes 4456448 | tf_op jit(solution)/shard_map/reduce_scatter | solution.py:332
  1249.5 582.0 %copy-start.1 = (bf16[8,1024]{1,0:T(8,128)(2,1)S(1)}, bf16[8,1024]{1,0:T(8,128)(2,1)}, u32[]{:S(2)}) copy-start(bf16[8,1024]{1,0:T(8,128)(2,1)} %param.17) | copy-start | bytes 49156
  (1 other events, 0.7 us)
Sparse Core Ops, SparseCore 0:
  10.2 53.2 all-gather.11
  65.7 39.8 all-gather.17
  107.7 40.1 all-gather.13
  150.0 140.7 all-gather.15
  292.8 66.6 all-gather.21
  361.5 38.4 all-gather.27
  402.1 39.0 all-gather.25
  443.3 41.3 all-gather.19
  486.9 73.6 all-gather.23
  695.9 35.8 reduce-scatter.22
  734.1 37.5 reduce-scatter.24
  787.4 9.7 reduce-scatter.58
  799.4 31.8 reduce-scatter.38
  833.4 31.8 reduce-scatter.34
  867.4 31.8 reduce-scatter.26
  901.4 31.8 reduce-scatter.30
  935.4 54.3 reduce-scatter.54
  992.0 54.2 reduce-scatter.50
  1048.6 99.2 reduce-scatter.42
  1150.2 99.2 reduce-scatter.46
  1253.5 55.0 reduce-scatter.60
  1312.2 56.4 reduce-scatter.40
  1372.7 56.3 reduce-scatter.36
  1432.7 56.4 reduce-scatter.28
  1493.2 56.3 reduce-scatter.32
  1553.2 60.5 reduce-scatter.56
  1617.9 60.4 reduce-scatter.52
  1682.3 71.4 reduce-scatter.44
  1758.2 71.4 reduce-scatter.48
